TPU v7x, 32 devices: a whole 2x2x4 slice. The times are simulated.
32 devices in a mesh: groups: 2 (over y), rows: 4 (over z), blocks: 2 (over x), cols: 2 (over core).
Axes of the slice: x: 2, y: 2, z: 4, core: 2. Of those that a mesh axis runs over, the one named last changes fastest.
Arguments:
- inputs: bfloat16 [4096, 1024], P(('groups', 'rows')), parts along dimension 0, may hold values from -6 to 6
- projection: bfloat16 [1024, 8192], P(None, ('groups', 'blocks', 'cols')), parts along dimension 1, may hold values from -0.1875 to 0.1875
- phases: bfloat16 [8192], P(('groups', 'blocks', 'cols')), parts along dimension 0, may hold values from -3.140625 to 3.140625
- inverse_blocks: float32 [4, 2048, 2048], P(('groups', 'blocks'), 'rows'), parts along dimension 0, as said below
- labels: int32 [4096], P(('groups', 'rows')), parts along dimension 0, may hold values from 0 to 999
- predictions: float32 [4096, 1000], P(('groups', 'rows'), 'cols'), parts along dimension 0, may hold values from -4 to 4
- coefficients: float32 [8192, 1000], P(('groups', 'blocks', 'rows'), 'cols'), parts along dimension 0, may hold values from -3 to 3
Outputs:
- new_coefficients: float32 [8192, 1000], P(('groups', 'blocks', 'rows'), 'cols'), parts along dimension 0
- new_predictions: float32 [4096, 1000], P(('groups', 'rows'), 'cols'), parts along dimension 0
There are 2 independent parts, one for each index of `groups`. A program takes and returns all parts, laid end to end along the dimension named above; each array names one. Nothing has to cross between parts.
Inputs may be any that keep to these rules, and one draw needn't show every extreme that they name: `inverse_blocks`: one dense preconditioner for each feature block.
All inputs are finite; a program needn't handle non-finite values.
Results may differ from a plain program's by a relative error of at most 0.0029.
Values may be sent and summed in bfloat16 or wider, within the bound.
No kernel may reach another device: no remote copies, remote signals or barrier semaphores. Data moves between devices by JAX's collectives and lax.ppermute only.
A program may use at most 64 MiB of HBM per device.

v0:
```python
import jax
import jax.numpy as jnp
from jax import lax
from jax.sharding import PartitionSpec as P

DAMPING = 0.5


def cosine_features(inputs, projection, phases):
    angles = (
        jnp.dot(inputs, projection, preferred_element_type=jnp.float32)
        + phases.astype(jnp.float32)[None, :]
    )
    return jnp.cos(angles).astype(jnp.bfloat16)


def shards(inputs, projection, phases, inverse_blocks, labels, predictions, coefficients):
    out_width = predictions.shape[1]
    classes = lax.axis_index("cols") * out_width + jnp.arange(out_width, dtype=jnp.int32)
    onehot = (labels[:, None] == classes[None, :]).astype(jnp.float32)
    residual = (onehot - predictions).astype(jnp.bfloat16)
    half_features = cosine_features(inputs, projection, phases)
    features_full = lax.all_gather(half_features, "cols", axis=1, tiled=True)
    local_inverse = inverse_blocks[0]
    column_slice = features_full
    own_gradient = lax.psum_scatter(
        lax.dot_general(
            column_slice, residual, (((0,), (0,)), ((), ())), preferred_element_type=jnp.float32
        ),
        "rows",
        scatter_dimension=0,
        tiled=True,
    )
    gradient = lax.all_gather(own_gradient, "rows", axis=0, tiled=True)
    solved = jnp.dot(local_inverse, gradient, precision=lax.Precision.HIGHEST)
    step_update = DAMPING * solved
    new_coefficients = coefficients + step_update
    column_slice = features_full
    contribution = jnp.dot(
        column_slice,
        lax.all_gather(step_update.astype(jnp.bfloat16), "rows", axis=0, tiled=True),
        preferred_element_type=jnp.float32,
    )
    summed = lax.psum(contribution, "blocks")
    return (new_coefficients, predictions + summed)


def solution(mesh):
    return jax.shard_map(
        shards,
        mesh=mesh,
        in_specs=(
            P(("groups", "rows"), None),
            P(None, ("groups", "blocks", "cols")),
            P(("groups", "blocks", "cols")),
            P(("groups", "blocks"), "rows", None),
            P(("groups", "rows")),
            P(("groups", "rows"), "cols"),
            P(("groups", "blocks", "rows"), "cols"),
        ),
        out_specs=(P(("groups", "blocks", "rows"), "cols"), P(("groups", "rows"), "cols")),
        check_vma=False,
    )
```

profile of v0, /device:TPU:0, one launch (start us, length us, event | category | flops | bytes accessed | tf_op | source)
XLA Modules:
  0.0 311.2 jit_solution(1773116370345842166)
XLA Ops:
  7.2 0.0 copy-start
  7.2 0.0 all-gather.4.cloned.1.call-start
  7.2 0.8 convert_element_type.15
  8.0 0.7 copy-done
  8.8 0.0 copy-start.1
  8.8 0.0 copy-start.2
  8.8 9.8 %cosine_convert_fusion = bf16[512,1024]{1,0:T(8,128)(2,1)} fusion(bf16[512,1024]{1,0:T(8,128)(2,1)} %param.7, bf16[1024,1024]{1,0:T(8,128)(2,1)S(1)} %copy-done, f32[1024]{0:T(1024)S(1)} %convert_element_type.15), kind=kOutput, calls=%fused_computation.2 | convolution fusion | flops 1074790400 | bytes 4198400 | tf_op jit(solution)/shard_map/dot_general | solution.py:11
  18.6 0.0 all-gather.4.cloned.1.call-update
  18.6 0.0 reduce-scatter.2.cloned.1.call-start
  18.7 13.4 %all-gather.4.cloned.1.call-done = bf16[512,2048]{1,0:T(8,128)(2,1)} async-done(((bf16[512,1024]{1,0:T(8,128)(2,1)}), bf16[512,2048]{1,0:T(8,128)(2,1)}) %all-gather.4.cloned.1.call-update) | async-done | bytes 2097168 | tf_op jit(solution)/shard_map/all_gather | solution.py:23
  32.1 0.0 copy-done.1
  32.1 0.0 copy-done.2
  32.1 5.0 %fusion.8 = f32[2048,500]{1,0:T(8,128)} fusion(bf16[512,2048]{1,0:T(8,128)(2,1)} %all-gather.4.cloned.1.call-done, f32[512,500]{0,1:T(8,128)S(1)} %copy-done.1, s32[512]{0:T(512)S(1)} %copy-done.2, s32[500]{0:T(512)S(1)} %iota_add_fusion), kind=kOutput, calls=%fused_computation.6 | convolution fusion | flops 1049600000 | bytes 7221200 | tf_op jit(solution)/shard_map/dot_general | solution.py:27
  37.0 0.0 reduce-scatter.2.cloned.1.call-update
  37.0 0.0 all-gather.6.cloned.1.call-start
  37.1 78.0 %reduce-scatter.2.cloned.1.call-done = f32[512,500]{1,0:T(8,128)} async-done(((f32[2048,500]{1,0:T(8,128)}), f32[512,500]{1,0:T(8,128)}) %reduce-scatter.2.cloned.1.call-update) | async-done | bytes 1024016 | tf_op jit(solution)/shard_map/reduce_scatter | solution.py:26
  115.1 0.0 all-gather.6.cloned.1.call-update
  115.2 0.2 all-gather.8.cloned.1.call-start
  115.4 82.7 %all-gather.6.cloned.1.call-done = f32[2048,500]{1,0:T(8,128)} async-done(((f32[512,500]{1,0:T(8,128)}), f32[2048,500]{1,0:T(8,128)}) %all-gather.6.cloned.1.call-update) | async-done | bytes 4096016 | tf_op jit(solution)/shard_map/all_gather | solution.py:34
  198.1 17.2 %fusion.11 = (bf16[512,500]{0,1:T(8,128)(2,1)}, f32[512,500]{0,1:T(8,128)}) fusion(f32[512,500]{0,1:T(8,128)} %param.13, f32[2048,500]{1,0:T(8,128)} %all-gather.6.cloned.1.call-done, f32[1,512,2048]{2,1,0:T(8,128)} %param.10), kind=kOutput, calls=%fused_computation.10 | convolution fusion | flops 6292224000 | bytes 10850304 | tf_op jit(solution)/shard_map/dot_general | solution.py:35
  215.3 0.0 all-gather.8.cloned.1.call-update
  215.3 0.0 all-reduce.2.cloned.1.call-start
  215.4 43.9 %all-gather.8.cloned.1.call-done = bf16[2048,500]{0,1:T(8,128)(2,1)} async-done(((bf16[512,500]{0,1:T(8,128)(2,1)}), bf16[2048,500]{0,1:T(8,128)(2,1)}) %all-gather.8.cloned.1.call-update) | async-done | bytes 2048016 | tf_op jit(solution)/shard_map/all_gather | solution.py:41
  259.3 4.4 %fusion.12 = f32[512,500]{0,1:T(8,128)} fusion(bf16[512,2048]{1,0:T(8,128)(2,1)} %all-gather.4.cloned.1.call-done, bf16[2048,500]{0,1:T(8,128)(2,1)} %all-gather.8.cloned.1.call-done), kind=kOutput, calls=%fused_computation.11 | convolution fusion | flops 1048576000 | bytes 5169152 | tf_op jit(solution)/shard_map/dot_general | solution.py:39
  263.7 0.0 all-reduce.2.cloned.1.call-update
  263.8 38.6 %all-reduce.2.cloned.1.call-done = f32[512,500]{0,1:T(8,128)} async-done(((f32[512,500]{0,1:T(8,128)}), f32[512,500]{0,1:T(8,128)}) %all-reduce.2.cloned.1.call-update) | async-done | bytes 1024016 | tf_op jit(solution)/shard_map/psum | solution.py:44
  302.3 2.4 add.33
  (1 shorter events, 0.0 us)
Async XLA Ops:
  7.2 1.6 copy-start
  7.2 24.9 %all-gather.4.cloned.1.call-start = ((), (), s32[]{:S(2)}) async-start(), calls=%async_computation.1 | async-start | bytes 3145728 | tf_op jit(solution)/shard_map/all_gather | solution.py:23
  8.8 23.3 %copy-start.1 = (f32[512,500]{0,1:T(8,128)S(1)}, f32[512,500]{0,1:T(8,128)}, u32[]{:S(2)}) copy-start(f32[512,500]{0,1:T(8,128)} %param.12) | copy-start | bytes 3072004
  8.8 23.3 %copy-start.2 = (s32[512]{0:T(512)S(1)}, s32[512]{0:T(512)}, u32[]{:S(2)}) copy-start(s32[512]{0:T(512)} %param.11) | copy-start | bytes 6148
  18.6 96.5 %reduce-scatter.2.cloned.1.call-start = ((), (), s32[]{:S(2)}) async-start(), calls=%async_computation.2 | async-start | bytes 5242880 | tf_op jit(solution)/shard_map/reduce_scatter | solution.py:26
  37.0 161.1 %all-gather.6.cloned.1.call-start = ((), (), s32[]{:S(2)}) async-start(), calls=%async_computation.3 | async-start | bytes 5242880 | tf_op jit(solution)/shard_map/all_gather | solution.py:34
  115.2 144.1 %all-gather.8.cloned.1.call-start = ((), (), s32[]{:S(2)}) async-start(), calls=%async_computation.4 | async-start | bytes 2580480 | tf_op jit(solution)/shard_map/all_gather | solution.py:41
  215.3 87.0 %all-reduce.2.cloned.1.call-start = ((), (), s32[]{:S(2)}) async-start(), calls=%async_computation.5 | async-start | bytes 2064384 | tf_op jit(solution)/shard_map/psum | solution.py:44
Sparse Core Ops, SparseCore 0:
  18.7 13.2 all-gather.3
  37.2 77.9 reduce-scatter.1
  116.8 81.2 all-gather.5
  215.4 43.8 all-gather.7
  263.9 38.3 all-reduce.1
where the time goes:
time: 311 us
  waiting for transfers between devices  257 us (83%)
  matrix products  36.4 us (12%)
  between operations  13.8 us (4%)
  other arithmetic  3.21 us (1%)
    all_gather x1, waiting for transfers between devices, shards(): gradient = lax.all_gather(own_gradient, 'rows', axis=0, tiled=True)  82.7 us
    reduce_scatter x1, waiting for transfers between devices, shards(): lax.psum_scatter(lax.dot_general(column_slice, residual, (((0,), (0,)), (...  78 us
    all_gather x1, waiting for transfers between devices, shards(): lax.all_gather(step_update.astype(jnp.bfloat16), 'rows', axis=0, tiled=True)  43.9 us
    psum x1, waiting for transfers between devices, shards(): summed = lax.psum(contribution, 'blocks')  38.6 us
    dot_general x1, matrix products, shards(): solved = jnp.dot(local_inverse, gradient, precision=lax.Precision.HIGHEST)  17.2 us
    all_gather x1, waiting for transfers between devices, shards(): features_full = lax.all_gather(half_features, 'cols', axis=1, tiled=True)  13.4 us
    dot_general x1, matrix products, cosine_features(): jnp.dot(inputs, projection, preferred_element_type=jnp.float32)  9.81 us
  transfers between devices with their start and end apart: 5, of which 5 were waited for; matrix products, arithmetic and copies ran while one was open for 0% of the time, Pallas kernels for 0%

commit v1 on v0

--- a/solution.py
+++ b/solution.py
@@ -41,7 +41,7 @@
         lax.all_gather(step_update.astype(jnp.bfloat16), "rows", axis=0, tiled=True),
         preferred_element_type=jnp.float32,
     )
-    summed = lax.psum(contribution, "blocks")
+    summed = lax.all_gather(contribution, "blocks").sum(axis=0)
     return (new_coefficients, predictions + summed)
 
 

time: 311 us -> 314 us (level)
  waiting for transfers between devices: 257 us -> 250 us
  other arithmetic: 3.21 us -> 8.17 us
  local copies, waits for them, and re-layouts: 0.74 us -> 4.73 us
    psum x1 -> x0, waiting for transfers between devices: 38.6 us -> none  [shards(): summed = lax.psum(contribution, 'blocks')]
    all_gather x0 -> x1, waiting for transfers between devices: none -> 31.6 us  [shards(): summed = lax.all_gather(contribution, 'blocks').sum(axis=0)]
    reduce_sum x0 -> x1, other arithmetic: none -> 4.97 us  [shards(): summed = lax.all_gather(contribution, 'blocks').sum(axis=0)]
    all_gather x0 -> x1, local copies, waits for them, and re-layouts: none -> 3.99 us  [shards(): summed = lax.all_gather(contribution, 'blocks').sum(axis=0)]
where the time goes in v1:
time: 314 us; the launch traced here: 313 us
  waiting for transfers between devices  250 us (80%)
  matrix products  36.4 us (12%)
  between operations  13.8 us (4%)
  other arithmetic  8.17 us (3%)
  local copies, waits for them, and re-layouts  4.73 us (2%)
    all_gather x1, waiting for transfers between devices, shards(): gradient = lax.all_gather(own_gradient, 'rows', axis=0, tiled=True)  82.7 us
    reduce_scatter x1, waiting for transfers between devices, shards(): lax.psum_scatter(lax.dot_general(column_slice, residual, (((0,), (0,)), (...  78 us
    all_gather x1, waiting for transfers between devices, shards(): lax.all_gather(step_update.astype(jnp.bfloat16), 'rows', axis=0, tiled=True)  43.7 us
    all_gather x1, waiting for transfers between devices, shards(): summed = lax.all_gather(contribution, 'blocks').sum(axis=0)  31.6 us
    dot_general x1, matrix products, shards(): solved = jnp.dot(local_inverse, gradient, precision=lax.Precision.HIGHEST)  17.2 us
    all_gather x1, waiting for transfers between devices, shards(): features_full = lax.all_gather(half_features, 'cols', axis=1, tiled=True)  13.4 us
    dot_general x1, matrix products, cosine_features(): jnp.dot(inputs, projection, preferred_element_type=jnp.float32)  9.81 us
  transfers between devices with their start and end apart: 5, of which 5 were waited for; matrix products, arithmetic and copies ran while one was open for 0% of the time, Pallas kernels for 0%

profile of v1, /device:TPU:0, one launch (start us, length us, event | category | flops | bytes accessed | tf_op | source)
XLA Modules:
  0.0 313.3 jit_solution(4050914878520662651)
XLA Ops:
  7.2 0.0 copy-start
  7.2 0.0 all-gather.6.cloned.1.call-start
  7.2 0.8 convert_element_type.15
  8.0 0.7 copy-done
  8.8 0.0 copy-start.1
  8.8 0.0 copy-start.2
  8.8 9.8 %cosine_convert_fusion = bf16[512,1024]{1,0:T(8,128)(2,1)} fusion(bf16[512,1024]{1,0:T(8,128)(2,1)} %param.7, bf16[1024,1024]{1,0:T(8,128)(2,1)S(1)} %copy-done, f32[1024]{0:T(1024)S(1)} %convert_element_type.15), kind=kOutput, calls=%fused_computation.2 | convolution fusion | flops 1074790400 | bytes 4198400 | tf_op jit(solution)/shard_map/dot_general | solution.py:11
  18.6 0.0 all-gather.6.cloned.1.call-update
  18.6 0.0 reduce-scatter.2.cloned.1.call-start
  18.7 13.4 %all-gather.6.cloned.1.call-done = bf16[512,2048]{1,0:T(8,128)(2,1)} async-done(((bf16[512,1024]{1,0:T(8,128)(2,1)}), bf16[512,2048]{1,0:T(8,128)(2,1)}) %all-gather.6.cloned.1.call-update) | async-done | bytes 2097168 | tf_op jit(solution)/shard_map/all_gather | solution.py:23
  32.1 0.0 copy-done.1
  32.1 0.0 copy-done.2
  32.1 5.0 %fusion.8 = f32[2048,500]{1,0:T(8,128)} fusion(bf16[512,2048]{1,0:T(8,128)(2,1)} %all-gather.6.cloned.1.call-done, f32[512,500]{0,1:T(8,128)S(1)} %copy-done.1, s32[512]{0:T(512)S(1)} %copy-done.2, s32[500]{0:T(512)S(1)} %iota_add_fusion), kind=kOutput, calls=%fused_computation.6 | convolution fusion | flops 1049600000 | bytes 7221200 | tf_op jit(solution)/shard_map/dot_general | solution.py:27
  37.0 0.0 reduce-scatter.2.cloned.1.call-update
  37.0 0.0 all-gather.8.cloned.1.call-start
  37.1 78.0 %reduce-scatter.2.cloned.1.call-done = f32[512,500]{1,0:T(8,128)} async-done(((f32[2048,500]{1,0:T(8,128)}), f32[512,500]{1,0:T(8,128)}) %reduce-scatter.2.cloned.1.call-update) | async-done | bytes 1024016 | tf_op jit(solution)/shard_map/reduce_scatter | solution.py:26
  115.1 0.0 all-gather.8.cloned.1.call-update
  115.2 0.2 all-gather.10.cloned.1.call-start
  115.4 82.7 %all-gather.8.cloned.1.call-done = f32[2048,500]{1,0:T(8,128)} async-done(((f32[512,500]{1,0:T(8,128)}), f32[2048,500]{1,0:T(8,128)}) %all-gather.8.cloned.1.call-update) | async-done | bytes 4096016 | tf_op jit(solution)/shard_map/all_gather | solution.py:34
  198.1 17.2 %fusion.11 = (bf16[512,500]{0,1:T(8,128)(2,1)}, f32[512,500]{0,1:T(8,128)}) fusion(f32[512,500]{0,1:T(8,128)} %param.13, f32[2048,500]{1,0:T(8,128)} %all-gather.8.cloned.1.call-done, f32[1,512,2048]{2,1,0:T(8,128)} %param.10), kind=kOutput, calls=%fused_computation.10 | convolution fusion | flops 6292224000 | bytes 10850304 | tf_op jit(solution)/shard_map/dot_general | solution.py:35
  215.3 0.0 all-gather.10.cloned.1.call-update
  215.3 0.3 all-gather.12.cloned.1.call-start
  215.6 43.7 %all-gather.10.cloned.1.call-done = bf16[2048,500]{0,1:T(8,128)(2,1)} async-done(((bf16[512,500]{0,1:T(8,128)(2,1)}), bf16[2048,500]{0,1:T(8,128)(2,1)}) %all-gather.10.cloned.1.call-update) | async-done | bytes 2048016 | tf_op jit(solution)/shard_map/all_gather | solution.py:41
  259.3 4.4 %fusion.12 = f32[512,500]{0,1:T(8,128)} fusion(bf16[512,2048]{1,0:T(8,128)(2,1)} %all-gather.6.cloned.1.call-done, bf16[2048,500]{0,1:T(8,128)(2,1)} %all-gather.10.cloned.1.call-done), kind=kOutput, calls=%fused_computation.11 | convolution fusion | flops 1048576000 | bytes 5169152 | tf_op jit(solution)/shard_map/dot_general | solution.py:39
  263.7 0.0 all-gather.12.cloned.1.call-update
  263.8 31.6 %all-gather.12.cloned.1.call-done = f32[1024,500]{0,1:T(8,128)} async-done(((f32[512,500]{0,1:T(8,128)}), f32[1024,500]{0,1:T(8,128)}) %all-gather.12.cloned.1.call-update) | async-done | bytes 2048016 | tf_op jit(solution)/shard_map/all_gather | solution.py:44
  295.4 4.0 %reshape.10 = f32[2,512,500]{1,0,2:T(2,128)} reshape(f32[1024,500]{0,1:T(8,128)} %all-gather.12.cloned.1.call-done) | data formatting | bytes 4096000 | tf_op jit(solution)/shard_map/all_gather | solution.py:44
  299.4 5.0 %reduce_sum.9 = f32[512,500]{0,1:T(8,128)} reduce(f32[2,512,500]{1,0,2:T(2,128)} %reshape.10, f32[]{:T(128)} %constant.3.clone.1), dimensions={0}, to_apply=%region_1.0 | reduce | flops 256000 | bytes 3072004 | tf_op jit(solution)/shard_map/reduce_sum | solution.py:44
  304.3 2.4 add.31
  (1 shorter events, 0.0 us)
Async XLA Ops:
  7.2 1.6 copy-start
  7.2 24.9 %all-gather.6.cloned.1.call-start = ((), (), s32[]{:S(2)}) async-start(), calls=%async_computation.1 | async-start | bytes 3145728 | tf_op jit(solution)/shard_map/all_gather | solution.py:23
  8.8 23.3 %copy-start.1 = (f32[512,500]{0,1:T(8,128)S(1)}, f32[512,500]{0,1:T(8,128)}, u32[]{:S(2)}) copy-start(f32[512,500]{0,1:T(8,128)} %param.12) | copy-start | bytes 3072004
  8.8 23.3 %copy-start.2 = (s32[512]{0:T(512)S(1)}, s32[512]{0:T(512)}, u32[]{:S(2)}) copy-start(s32[512]{0:T(512)} %param.11) | copy-start | bytes 6148
  18.6 96.5 %reduce-scatter.2.cloned.1.call-start = ((), (), s32[]{:S(2)}) async-start(), calls=%async_computation.2 | async-start | bytes 5242880 | tf_op jit(solution)/shard_map/reduce_scatter | solution.py:26
  37.0 161.1 %all-gather.8.cloned.1.call-start = ((), (), s32[]{:S(2)}) async-start(), calls=%async_computation.3 | async-start | bytes 5242880 | tf_op jit(solution)/shard_map/all_gather | solution.py:34
  115.2 144.1 %all-gather.10.cloned.1.call-start = ((), (), s32[]{:S(2)}) async-start(), calls=%async_computation.4 | async-start | bytes 2580480 | tf_op jit(solution)/shard_map/all_gather | solution.py:41
  215.3 80.1 %all-gather.12.cloned.1.call-start = ((), (), s32[]{:S(2)}) async-start(), calls=%async_computation.5 | async-start | bytes 3096576 | tf_op jit(solution)/shard_map/all_gather | solution.py:44
Sparse Core Ops, SparseCore 0:
  18.7 13.2 all-gather.5
  37.2 77.9 reduce-scatter.1
  116.8 81.2 all-gather.7
  215.4 43.8 all-gather.9
  263.9 31.4 all-gather.11
